TPU v7x, 32 devices: a whole 2x2x4 slice. The times are simulated.
32 devices in a mesh: seq: 4 (over y, x), ctx: 8 (over z, core).
Axes of the slice: x: 2, y: 2, z: 4, core: 2. Of those that a mesh axis runs over, the one named last changes fastest.
Arguments:
- inputs: bfloat16 [4096, 1152], P(('seq', 'ctx')), may hold values from -140 to 140
- positions: int32 [4096], P(('seq', 'ctx')), may hold values from 0 to 1023, as said below
- attention_gain: bfloat16 [1152], P(('seq', 'ctx')), may hold values from 0.3984375 to 1.59375
- query_weight: bfloat16 [1152, 1024], P(('seq', 'ctx')), may hold values from -0.1875 to 0.1875
- key_weight: bfloat16 [1152, 256], P(('seq', 'ctx')), may hold values from -0.1875 to 0.1875
- value_weight: bfloat16 [1152, 256], P(('seq', 'ctx')), may hold values from -0.1875 to 0.1875
- query_gain: bfloat16 [256], P(('seq', 'ctx')), may hold values from 0.5 to 1.5
- key_gain: bfloat16 [256], P(('seq', 'ctx')), may hold values from 0.5 to 1.5
- output_weight: bfloat16 [1024, 1152], P(('seq', 'ctx')), may hold values from -0.1875 to 0.1875
- attention_post: bfloat16 [1152], P(('seq', 'ctx')), may hold values from 0.3984375 to 1.59375
- feedfwd_gain: bfloat16 [1152], P(('seq', 'ctx')), may hold values from 0.3984375 to 1.59375
- gate_weight: bfloat16 [1152, 6912], P(('seq', 'ctx')), may hold values from -0.1875 to 0.1875
- up_weight: bfloat16 [1152, 6912], P(('seq', 'ctx')), may hold values from -0.1875 to 0.1875
- down_weight: bfloat16 [6912, 1152], P(('seq', 'ctx')), may hold values from -0.078125 to 0.078125
- feedfwd_post: bfloat16 [1152], P(('seq', 'ctx')), may hold values from 0.3984375 to 1.59375
- cotangent: bfloat16 [4096, 1152], P(('seq', 'ctx')), may hold values from -6 to 6
Outputs:
- block_out: bfloat16 [4096, 1152], P(('seq', 'ctx'))
- input_grad: float32 [4096, 1152], P(('seq', 'ctx'))
- attention_gain_grad: float32 [1152], P(('seq', 'ctx'))
- query_grad: float32 [1152, 1024], P(('seq', 'ctx'))
- key_grad: float32 [1152, 256], P(('seq', 'ctx'))
- value_grad: float32 [1152, 256], P(('seq', 'ctx'))
- query_gain_grad: float32 [256], P(('seq', 'ctx'))
- key_gain_grad: float32 [256], P(('seq', 'ctx'))
- output_grad: float32 [1024, 1152], P(('seq', 'ctx'))
- attention_post_grad: float32 [1152], P(('seq', 'ctx'))
- feedfwd_gain_grad: float32 [1152], P(('seq', 'ctx'))
- gate_grad: float32 [1152, 6912], P(('seq', 'ctx'))
- up_grad: float32 [1152, 6912], P(('seq', 'ctx'))
- down_grad: float32 [6912, 1152], P(('seq', 'ctx'))
- feedfwd_post_grad: float32 [1152], P(('seq', 'ctx'))
Inputs may be any that keep to these rules, and one draw needn't show every extreme that they name: Within each sequence of 1024 tokens, the 128 tokens of each ctx index hold the consecutive positions k * 128 to k * 128 + 127, where the block numbers k of one sequence's ctx indices are a permutation of 0 to 7, drawn afresh for every sequence.
All inputs are finite; a program needn't handle non-finite values.
Results may differ from a plain program's by a relative error of at most 0.038.
Values may be sent and summed in bfloat16 or wider, within the bound.
A program may use at most 448 MiB of HBM per device.

v0:
```python
import math

import jax
import jax.numpy as jnp
from jax import lax
from jax.sharding import PartitionSpec as P

D = 1152
H = 4
DH = 256
FF = 6912


EPSILON = 1e-06
THETA = 1000000.0
GELU_COEF = math.sqrt(2.0 / math.pi)


def rms_factor(values):
    return lax.rsqrt(jnp.mean(values * values, axis=-1, keepdims=True) + EPSILON)


def norm_back(values, factor, gain_vector, upstream):
    scaled = gain_vector * upstream
    cubed = factor * factor * factor
    return factor * scaled - values * cubed * jnp.mean(scaled * values, axis=-1, keepdims=True)


def rotary(places):
    half_width = DH // 2
    exponent = jnp.arange(half_width, dtype=jnp.float32) * (-2.0 / DH)
    frequency = jnp.power(jnp.float32(THETA), exponent)
    angles = places.astype(jnp.float32)[:, None] * frequency[None, :]
    return (jnp.cos(angles), jnp.sin(angles))


def rotate(values, cosine, sinus):
    half_width = values.shape[-1] // 2
    first = values[..., :half_width]
    second = values[..., half_width:]
    return jnp.concatenate(
        [first * cosine - second * sinus, second * cosine + first * sinus], axis=-1
    )


def rotate_back(upstream, cosine, sinus):
    half_width = upstream.shape[-1] // 2
    first = upstream[..., :half_width]
    second = upstream[..., half_width:]
    return jnp.concatenate(
        [first * cosine + second * sinus, second * cosine - first * sinus], axis=-1
    )


def gelu_tanh(values):
    inner = GELU_COEF * (values + 0.044715 * values * values * values)
    return 0.5 * values * (1.0 + jnp.tanh(inner))


def gelu_slope(values):
    inner = GELU_COEF * (values + 0.044715 * values * values * values)
    tangent = jnp.tanh(inner)
    return 0.5 * (1.0 + tangent) + 0.5 * values * (1.0 - tangent * tangent) * GELU_COEF * (
        1.0 + 3.0 * 0.044715 * values * values
    )


def times_right(left_side, right_side):
    return jnp.dot(left_side, right_side, preferred_element_type=jnp.float32)


def times_transposed(left_side, right_side):
    return lax.dot_general(
        left_side, right_side, (((1,), (1,)), ((), ())), preferred_element_type=jnp.float32
    )


def transposed_times(left_side, right_side):
    return lax.dot_general(
        left_side, right_side, (((0,), (0,)), ((), ())), preferred_element_type=jnp.float32
    )


def attend_back(
    query_part, place_part, output_part, logsum_part, upper_part, key_all, value_all, place_all
):
    scaling = 1.0 / math.sqrt(DH)
    upper_round = upper_part.astype(jnp.bfloat16)
    row_delta = jnp.sum(upper_part * output_part.astype(jnp.float32), axis=-1)
    scores = (
        jnp.einsum("qhd,kd->hqk", query_part, key_all, preferred_element_type=jnp.float32) * scaling
    )
    allowed = place_all[None, None, :] <= place_part[None, :, None]
    probability = jnp.where(allowed, jnp.exp(scores - jnp.transpose(logsum_part)[:, :, None]), 0.0)
    value_sum = jnp.einsum(
        "hqk,qhd->kd",
        probability.astype(jnp.bfloat16),
        upper_round,
        preferred_element_type=jnp.float32,
    )
    prob_back = jnp.einsum(
        "qhd,kd->hqk", upper_round, value_all, preferred_element_type=jnp.float32
    )
    score_back = (
        probability * (prob_back - jnp.transpose(row_delta)[:, :, None]) * scaling
    ).astype(jnp.bfloat16)
    query_back = jnp.einsum("hqk,kd->qhd", score_back, key_all, preferred_element_type=jnp.float32)
    key_back = jnp.einsum("hqk,qhd->kd", score_back, query_part, preferred_element_type=jnp.float32)
    return (query_back, key_back, value_sum)


def per_device(
    inputs,
    positions,
    attention_gain,
    query_weight,
    key_weight,
    value_weight,
    query_gain,
    key_gain,
    output_weight,
    attention_post,
    feedfwd_gain,
    gate_weight,
    up_weight,
    down_weight,
    feedfwd_post,
    cotangent,
):
    attention_set = (
        lax.all_gather(attention_gain, ("seq", "ctx"), axis=0, tiled=True),
        lax.all_gather(query_weight, ("seq", "ctx"), axis=0, tiled=True),
        lax.all_gather(key_weight, ("seq", "ctx"), axis=0, tiled=True),
        lax.all_gather(value_weight, ("seq", "ctx"), axis=0, tiled=True),
        lax.all_gather(query_gain, ("seq", "ctx"), axis=0, tiled=True),
        lax.all_gather(key_gain, ("seq", "ctx"), axis=0, tiled=True),
        lax.all_gather(output_weight, ("seq", "ctx"), axis=0, tiled=True),
        lax.all_gather(attention_post, ("seq", "ctx"), axis=0, tiled=True),
    )
    feedfwd_set = (
        lax.all_gather(feedfwd_gain, ("seq", "ctx"), axis=0, tiled=True),
        lax.all_gather(gate_weight, ("seq", "ctx"), axis=0, tiled=True),
        lax.all_gather(up_weight, ("seq", "ctx"), axis=0, tiled=True),
        lax.all_gather(down_weight, ("seq", "ctx"), axis=0, tiled=True),
        lax.all_gather(feedfwd_post, ("seq", "ctx"), axis=0, tiled=True),
    )
    gain_attention = attention_set[0].astype(jnp.float32)
    gain_query = attention_set[4].astype(jnp.float32)
    gain_key = attention_set[5].astype(jnp.float32)
    gain_post = attention_set[7].astype(jnp.float32)
    gain_feed = feedfwd_set[0].astype(jnp.float32)
    gain_final = feedfwd_set[4].astype(jnp.float32)
    token_count = inputs.shape[0]
    scaling = 1.0 / math.sqrt(DH)
    device_total = lax.axis_size(("seq", "ctx"))
    input_wide = inputs.astype(jnp.float32)
    input_factor = rms_factor(input_wide)
    normed = (input_wide * input_factor * gain_attention).astype(jnp.bfloat16)
    queries = times_right(normed, attention_set[1]).reshape(token_count, H, DH)
    key_rows = times_right(normed, attention_set[2])
    value_rows = times_right(normed, attention_set[3]).astype(jnp.bfloat16)
    cosine, sinus = rotary(positions)
    query_factor = rms_factor(queries)
    query_rot = rotate(
        queries * query_factor * gain_query, cosine[:, None, :], sinus[:, None, :]
    ).astype(jnp.bfloat16)
    key_factor = rms_factor(key_rows)
    key_rot = rotate(key_rows * key_factor * gain_key, cosine, sinus).astype(jnp.bfloat16)
    key_piece = lax.all_gather(key_rot, "ctx", axis=0, tiled=True)
    value_piece = lax.all_gather(value_rows, "ctx", axis=0, tiled=True)
    place_piece = lax.all_gather(positions, "ctx", axis=0, tiled=True)
    scores = (
        jnp.einsum("qhd,kd->hqk", query_rot, key_piece, preferred_element_type=jnp.float32)
        * scaling
    )
    allowed = place_piece[None, None, :] <= positions[None, :, None]
    expscore = jnp.where(allowed, jnp.exp(scores), 0.0)
    weight_sum = jnp.sum(expscore, axis=-1)
    summed = jnp.einsum(
        "hqk,kd->qhd",
        expscore.astype(jnp.bfloat16),
        value_piece,
        preferred_element_type=jnp.float32,
    )
    weight_sum, summed = (weight_sum, summed)
    attended_heads = (summed / jnp.transpose(weight_sum)[:, :, None]).astype(jnp.bfloat16)
    logsum = jnp.transpose(jnp.log(weight_sum))
    attended = attended_heads.reshape(token_count, H * DH)
    mixed_values = times_right(attended, attention_set[6])
    mixed_factor = rms_factor(mixed_values)
    residual = input_wide + mixed_values * mixed_factor * gain_post
    residual_factor = rms_factor(residual)
    fed_rows = (residual * residual_factor * gain_feed).astype(jnp.bfloat16)
    gate_values = times_right(fed_rows, feedfwd_set[1])
    up_values = times_right(fed_rows, feedfwd_set[2])
    hidden = (gelu_tanh(gate_values) * up_values).astype(jnp.bfloat16)
    down_values = times_right(hidden, feedfwd_set[3])
    down_factor = rms_factor(down_values)
    block_out = (residual + down_values * down_factor * gain_final).astype(jnp.bfloat16)
    feedfwd_back = (
        lax.all_gather(feedfwd_gain, ("seq", "ctx"), axis=0, tiled=True),
        lax.all_gather(gate_weight, ("seq", "ctx"), axis=0, tiled=True),
        lax.all_gather(up_weight, ("seq", "ctx"), axis=0, tiled=True),
        lax.all_gather(down_weight, ("seq", "ctx"), axis=0, tiled=True),
        lax.all_gather(feedfwd_post, ("seq", "ctx"), axis=0, tiled=True),
    )
    cot_wide = cotangent.astype(jnp.float32)
    grad_final = jnp.sum(cot_wide * down_values * down_factor, axis=0)
    down_back = norm_back(down_values, down_factor, gain_final, cot_wide).astype(jnp.bfloat16)
    hidden_back = times_transposed(down_back, feedfwd_back[3])
    gate_back = (hidden_back * up_values * gelu_slope(gate_values)).astype(jnp.bfloat16)
    up_back = (hidden_back * gelu_tanh(gate_values)).astype(jnp.bfloat16)
    fed_back = times_transposed(gate_back, feedfwd_back[1]) + times_transposed(
        up_back, feedfwd_back[2]
    )
    grad_feed = jnp.sum(fed_back * residual * residual_factor, axis=0)
    residual_back = cot_wide + norm_back(residual, residual_factor, gain_feed, fed_back)
    grad_post = jnp.sum(residual_back * mixed_values * mixed_factor, axis=0)
    mixed_back = norm_back(mixed_values, mixed_factor, gain_post, residual_back).astype(
        jnp.bfloat16
    )
    out_share = H * DH // device_total
    down_share = FF // device_total
    column_share = out_share + down_share
    shard_count = column_share * lax.axis_size(("seq", "ctx")) // column_share
    out_term = transposed_times(attended, mixed_back).reshape(shard_count, out_share, D)
    down_term = transposed_times(hidden, down_back).reshape(shard_count, down_share, D)
    column_block = lax.psum_scatter(
        jnp.concatenate([out_term, down_term], axis=1).reshape(
            column_share * lax.axis_size(("seq", "ctx")), D
        ),
        ("seq", "ctx"),
        scatter_dimension=0,
        tiled=True,
    )
    grad_output = column_block[:out_share]
    grad_down = column_block[out_share:]
    attention_back = (
        lax.all_gather(attention_gain, ("seq", "ctx"), axis=0, tiled=True),
        lax.all_gather(query_weight, ("seq", "ctx"), axis=0, tiled=True),
        lax.all_gather(key_weight, ("seq", "ctx"), axis=0, tiled=True),
        lax.all_gather(value_weight, ("seq", "ctx"), axis=0, tiled=True),
        lax.all_gather(query_gain, ("seq", "ctx"), axis=0, tiled=True),
        lax.all_gather(key_gain, ("seq", "ctx"), axis=0, tiled=True),
        lax.all_gather(output_weight, ("seq", "ctx"), axis=0, tiled=True),
        lax.all_gather(attention_post, ("seq", "ctx"), axis=0, tiled=True),
    )
    attended_back = times_transposed(mixed_back, attention_back[6]).reshape(token_count, H, DH)
    key_all, value_all, place_all = (
        lax.all_gather(key_rot, "ctx", axis=0, tiled=True),
        lax.all_gather(value_rows, "ctx", axis=0, tiled=True),
        lax.all_gather(positions, "ctx", axis=0, tiled=True),
    )
    block_len = min(token_count, 128)
    block_count = token_count // block_len

    def back_block(state_now, pieces):
        query_part, place_part, output_part, logsum_part, upper_part = pieces
        query_back, key_back, value_sum = attend_back(
            query_part,
            place_part,
            output_part,
            logsum_part,
            upper_part,
            key_all,
            value_all,
            place_all,
        )
        return ((state_now[0] + key_back, state_now[1] + value_sum), query_back)

    zero_rows = jnp.zeros((key_all.shape[0], DH), jnp.float32)
    blocks_in = (
        query_rot.reshape(block_count, block_len, H, DH),
        positions.reshape(block_count, block_len),
        attended_heads.reshape(block_count, block_len, H, DH),
        logsum.reshape(block_count, block_len, H),
        attended_back.reshape(block_count, block_len, H, DH),
    )
    (key_terms, value_terms), query_parts = lax.scan(back_block, (zero_rows, zero_rows), blocks_in)
    own_rows = lax.psum_scatter(
        jnp.concatenate([key_terms, value_terms], axis=1).astype(jnp.bfloat16),
        "ctx",
        scatter_dimension=0,
        tiled=True,
    ).astype(jnp.float32)
    key_rot_back = own_rows[:, :DH]
    value_back = own_rows[:, DH:].astype(jnp.bfloat16)
    query_rot_back = query_parts.reshape(token_count, H, DH)
    query_up = rotate_back(query_rot_back, cosine[:, None, :], sinus[:, None, :])
    grad_qgain = jnp.sum(query_up * queries * query_factor, axis=(0, 1))
    query_back = (
        norm_back(queries, query_factor, gain_query, query_up)
        .astype(jnp.bfloat16)
        .reshape(token_count, H * DH)
    )
    key_up = rotate_back(key_rot_back, cosine, sinus)
    grad_kgain = jnp.sum(key_up * key_rows * key_factor, axis=0)
    key_back = norm_back(key_rows, key_factor, gain_key, key_up).astype(jnp.bfloat16)
    normed_back = (
        times_transposed(query_back, attention_back[1])
        + times_transposed(key_back, attention_back[2])
        + times_transposed(value_back, attention_back[3])
    )
    grad_attention = jnp.sum(normed_back * input_wide * input_factor, axis=0)
    input_grad = residual_back + norm_back(input_wide, input_factor, gain_attention, normed_back)
    attention_backs = jnp.concatenate([query_back, key_back, value_back], axis=1)
    feedfwd_backs = jnp.concatenate([gate_back, up_back], axis=1)
    row_block = lax.psum_scatter(
        jnp.concatenate(
            [transposed_times(normed, attention_backs), transposed_times(fed_rows, feedfwd_backs)],
            axis=1,
        ),
        ("seq", "ctx"),
        scatter_dimension=0,
        tiled=True,
    )
    grad_query = row_block[:, : H * DH]
    grad_key = row_block[:, H * DH : H * DH + DH]
    grad_value = row_block[:, H * DH + DH : H * DH + 2 * DH]
    grad_gate = row_block[:, H * DH + 2 * DH : H * DH + 2 * DH + FF]
    grad_up = row_block[:, H * DH + 2 * DH + FF :]
    gains_summed = (
        lax.psum_scatter(grad_attention, ("seq", "ctx"), scatter_dimension=0, tiled=True),
        lax.psum_scatter(grad_qgain, ("seq", "ctx"), scatter_dimension=0, tiled=True),
        lax.psum_scatter(grad_kgain, ("seq", "ctx"), scatter_dimension=0, tiled=True),
        lax.psum_scatter(grad_post, ("seq", "ctx"), scatter_dimension=0, tiled=True),
        lax.psum_scatter(grad_feed, ("seq", "ctx"), scatter_dimension=0, tiled=True),
        lax.psum_scatter(grad_final, ("seq", "ctx"), scatter_dimension=0, tiled=True),
    )
    return (
        block_out,
        input_grad,
        gains_summed[0],
        grad_query,
        grad_key,
        grad_value,
        gains_summed[1],
        gains_summed[2],
        grad_output,
        gains_summed[3],
        gains_summed[4],
        grad_gate,
        grad_up,
        grad_down,
        gains_summed[5],
    )


def solution(mesh):
    return jax.shard_map(
        per_device,
        mesh=mesh,
        in_specs=(
            P(("seq", "ctx"), None),
            P(("seq", "ctx")),
            P(("seq", "ctx")),
            P(("seq", "ctx"), None),
            P(("seq", "ctx"), None),
            P(("seq", "ctx"), None),
            P(("seq", "ctx")),
            P(("seq", "ctx")),
            P(("seq", "ctx"), None),
            P(("seq", "ctx")),
            P(("seq", "ctx")),
            P(("seq", "ctx"), None),
            P(("seq", "ctx"), None),
            P(("seq", "ctx"), None),
            P(("seq", "ctx")),
            P(("seq", "ctx"), None),
        ),
        out_specs=(
            P(("seq", "ctx"), None),
            P(("seq", "ctx"), None),
            P(("seq", "ctx")),
            P(("seq", "ctx"), None),
            P(("seq", "ctx"), None),
            P(("seq", "ctx"), None),
            P(("seq", "ctx")),
            P(("seq", "ctx")),
            P(("seq", "ctx"), None),
            P(("seq", "ctx")),
            P(("seq", "ctx")),
            P(("seq", "ctx"), None),
            P(("seq", "ctx"), None),
            P(("seq", "ctx"), None),
            P(("seq", "ctx")),
        ),
        check_vma=False,
    )
```

profile of v0, /device:TPU:0, one launch (start us, length us, event | category | flops | bytes accessed | tf_op | source)
XLA Modules:
  0.0 2184.6 jit_solution(18043881758278048469)
XLA Ops:
  16.4 42.4 %all-reduce.16 = (bf16[1152]{0:T(1024)(128)(2,1)S(1)}, bf16[256]{0:T(256)(128)(2,1)S(1)}, bf16[256]{0:T(256)(128)(2,1)S(1)}, bf16[1152]{0:T(1024)(128)(2,1)S(1)}...) all-reduce(bf16[1152]{0:T(1024)(128)(2,1)S(1)} %dynamic-update-slic, ...), channel_id=1, replica_groups=mesh['seq'=4,'ctx'=8] {'seq','ctx'}, use_global_device_ids=true, to_apply=%add | all-reduce | flops 5120 | bytes 20480
  60.6 43.6 %all-gather.2 = bf16[32,36,256]{2,1,0:T(8,128)(2,1)S(1)} all-gather(bf16[1,36,256]{2,1,0:T(8,128)(2,1)} %bitcast.148), channel_id=1, replica_groups=mesh['seq'=4,'ctx'=8] {'seq','ctx'}, dimensions={0}, use_global_device_ids=true | all-gather | bytes 608256 | tf_op jit(solution)/shard_map/all_gather | solution.py:133
  104.4 40.5 %all-gather = bf16[32,36,256]{2,1,0:T(8,128)(2,1)S(1)} all-gather(bf16[1,36,256]{2,1,0:T(8,128)(2,1)S(1)} %bitcast.149), channel_id=1, replica_groups=mesh['seq'=4,'ctx'=8] {'seq','ctx'}, dimensions={0}, use_global_device_ids=true | all-gather | bytes 608256 | tf_op jit(solution)/shard_map/all_gather | solution.py:134
  145.1 10.4 all-gather.1
  159.0 18.2 all_gather.64
  177.5 18.4 all_gather.60
  195.9 2.7 reshape.304
  199.2 1.0 reshape.281
  200.2 1.3 multiply_reduce_fusion.9
  202.0 0.9 copy.162
  203.2 0.9 copy.164
  206.8 2.4 multiply_reduce_fusion.6
  211.0 45.9 %all-gather.18.cloned.1.call-done = bf16[32,36,6912]{2,1,0:T(8,128)(2,1)} async-done(((bf16[1,36,6912]{2,1,0:T(8,128)(2,1)}), bf16[32,36,6912]{2,1,0:T(8,128)(2,1)}) %all-gather.18.cloned.1.call-update) | async-done | bytes 15925264 | tf_op jit(solution)/shard_map/all_gather | solution.py:142
  256.9 18.5 reshape.306
  275.3 101.3 %all-gather.20.cloned.1.call-done = bf16[32,36,6912]{2,1,0:T(8,128)(2,1)} async-done(((bf16[1,36,6912]{2,1,0:T(8,128)(2,1)}), bf16[32,36,6912]{2,1,0:T(8,128)(2,1)}) %all-gather.20.cloned.1.call-update) | async-done | bytes 15925264 | tf_op jit(solution)/shard_map/all_gather | solution.py:143
  376.6 18.6 reshape.308
  395.2 8.2 fusion.98
  403.5 1.8 copy-done.3
  405.3 1.4 copy-done
  406.6 4.6 multiply_convert_fusion.1
  411.3 77.0 %all-gather.14.cloned.1.call-done = bf16[6912,1152]{1,0:T(8,128)(2,1)} async-done(((bf16[216,1152]{1,0:T(8,128)(2,1)}), bf16[6912,1152]{1,0:T(8,128)(2,1)}) %all-gather.14.cloned.1.call-update) | async-done | bytes 15925264 | tf_op jit(solution)/shard_map/all_gather | solution.py:144
  488.3 8.2 multiply_reduce_fusion.4
  497.3 1.0 fusion.36
  498.3 10.4 multiply_convert_fusion
  508.8 11.2 fusion.99
  520.1 12.6 multiply_reduce_fusion
  532.7 2.3 multiply_reduce_fusion.1
  536.1 1.4 fusion.21
  539.0 1.2 fusion.20
  540.3 12.6 fusion.101
  552.9 25.1 %fusion.7 = f32[1152,13824]{1,0:T(8,128)} fusion(bf16[128,1152]{1,0:T(8,128)(2,1)S(1)} %multiply_convert_fusion.2, bf16[128,6912]{1,0:T(8,128)(2,1)} %get-tuple-element.82, bf16[128,6912]{1,0:T(8,128)(2,1)} %copy-done.9), kind=kOutput, calls=%fused_computation.11 | convolution fusion | flops 4083941376 | bytes 67534848 | tf_op jit(solution)/shard_map/dot_general | solution.py:79
  578.0 1.1 pad_maximum_fusion.2
  581.0 24.9 %pad_maximum_fusion.1 = f32[32,248,1152]{2,1,0:T(8,128)} fusion(f32[32,216,1152]{2,1,0:T(8,128)} %bitcast.130, f32[32,32,1152]{2,1,0:T(8,128)S(1)} %fusion.63), kind=kLoop, calls=%fused_computation.1 | loop fusion | flops 9142272 | bytes 73138176 | tf_op jit(solution)/shard_map/concatenate | solution.py:229
  605.9 4.2 reduce-scatter.2.cloned.1.call-done
  610.1 0.9 convert_element_type.115
  612.6 4.0 fusion.57
  616.6 47.3 %pad_maximum_fusion = f32[1152,15360]{1,0:T(8,128)} fusion(f32[1152,13824]{1,0:T(8,128)} %fusion.7, f32[1152,1536]{1,0:T(8,128)} %fusion.57), kind=kLoop, calls=%fused_computation | loop fusion | flops 17694720 | bytes 141557760 | tf_op jit(solution)/shard_map/concatenate | solution.py:309
  663.9 1.6 copy-done.2
  666.4 1.5 convolution_add_fusion.1
  667.9 1.6 fusion.48
  669.5 40.2 %all-reduce.14 = (f32[1152]{0:T(1024)S(1)}, f32[256]{0:T(256)S(1)}, f32[256]{0:T(256)S(1)}, f32[1152]{0:T(1024)S(1)}, f32[1152]{0:T(1024)S(1)}, /*index=5*/f32[1152]{0:T(1024)S(1)}) all-reduce(f32[1152]{0:T(1024)S(1)} %get-tuple-element.57, f32[256]{0:T(256)S(1)} %reduce_sum.205, ...), channel_id=3, replica_groups=mesh['seq'=4,'ctx'=8] {'seq','ctx'}, use_global_device_ids=true, to_apply=%region_16.17.clone | all-reduce | flops 5120 | bytes 40960
  713.3 1.1 fusion.45
  714.3 1452.1 %all-reduce.19.cloned.1.call-done = (f32[1152,15360]{1,0:T(8,128)}, f32[7936,1152]{1,0:T(8,128)}) async-done(((f32[1152,15360]{1,0:T(8,128)}, f32[7936,1152]{1,0:T(8,128)}), (f32[1152,15360]{1,0:T(8,128)}, f32[7936,1152]{1,0:T(8,128)})) %all-reduce.19.cloned.1.call-update) | async-done | bytes 107347984
  2166.5 1.6 constant_dynamic-slice_fusion
  2168.0 2.2 constant_dynamic-slice_fusion.2
  2170.3 1.6 constant_dynamic-slice_fusion.1
  2171.9 1.7 fusion.97
  2173.6 3.7 fusion.96
  (237 shorter events, 31.8 us)
Async XLA Ops:
  7.2 137.9 %copy-start.63 = (s32[128]{0:T(128)S(1)}, s32[128]{0:T(128)}, u32[]{:S(2)}) copy-start(s32[128]{0:T(128)} %param.17) | copy-start | bytes 1540
  7.2 97.2 %copy-start.45 = (bf16[36,256]{1,0:T(8,128)(2,1)S(1)}, bf16[36,256]{1,0:T(8,128)(2,1)}, u32[]{:S(2)}) copy-start(bf16[36,256]{1,0:T(8,128)(2,1)} %param.21) | copy-start | bytes 55300
  7.2 148.3 %copy-start.5 = (bf16[128,1152]{1,0:T(8,128)(2,1)S(1)}, bf16[128,1152]{1,0:T(8,128)(2,1)}, u32[]{:S(2)}) copy-start(bf16[128,1152]{1,0:T(8,128)(2,1)} %param.16) | copy-start | bytes 884740
  7.2 188.7 %all-gather.16.cloned.1.call-start = ((), (), s32[]{:S(2)}) async-start(), calls=%async_computation.4 | async-start | bytes 2703360 | tf_op jit(solution)/shard_map/all_gather | solution.py:132
  7.9 198.9 %all-gather.12.cloned.1.call-start = ((), (), s32[]{:S(2)}) async-start(), calls=%async_computation.1 | async-start | bytes 2433024 | tf_op jit(solution)/shard_map/all_gather | solution.py:137
  8.7 248.2 %all-gather.18.cloned.1.call-start = ((), (), s32[]{:S(2)}) async-start(), calls=%async_computation.5 | async-start | bytes 18247680 | tf_op jit(solution)/shard_map/all_gather | solution.py:142
  9.4 367.2 %all-gather.20.cloned.1.call-start = ((), (), s32[]{:S(2)}) async-start(), calls=%async_computation.6 | async-start | bytes 18247680 | tf_op jit(solution)/shard_map/all_gather | solution.py:143
  10.0 478.3 %all-gather.14.cloned.1.call-start = ((), (), s32[]{:S(2)}) async-start(), calls=%async_computation.2 | async-start | bytes 16422912 | tf_op jit(solution)/shard_map/all_gather | solution.py:144
  10.6 599.5 %reduce-scatter.2.cloned.1.call-start = ((), (), s32[]{:S(2)}) async-start(), calls=%async_computation.3 | async-start | bytes 1179648 | tf_op jit(solution)/shard_map/reduce_scatter | solution.py:280
  11.3 166.2 %copy-start.59 = (f32[128]{0:T(128)}, f32[128]{0:T(128)S(1)}, u32[]{:S(2)}) copy-start(f32[128]{0:T(128)S(1)} %convert_element_type.95) | copy-start | bytes 1540
  58.8 98.4 %copy-start.49 = (f32[256]{0:T(256)}, f32[256]{0:T(256)S(1)}, u32[]{:S(2)}) copy-start(f32[256]{0:T(256)S(1)} %convert_element_type.94) | copy-start | bytes 3076
  58.8 145.3 %copy-start.51 = (f32[256]{0:T(256)}, f32[256]{0:T(256)S(1)}, u32[]{:S(2)}) copy-start(f32[256]{0:T(256)S(1)} %convert_element_type.96) | copy-start | bytes 3076
  104.4 91.5 %copy-start.13 = (bf16[1152,256]{1,0:T(8,128)(2,1)}, bf16[1152,256]{1,0:T(8,128)(2,1)S(1)}, u32[]{:S(2)}) copy-start(bf16[1152,256]{1,0:T(8,128)(2,1)S(1)} %reshape.302) | copy-start | bytes 1769476
  145.0 50.9 %copy-start.14 = (bf16[1152,256]{1,0:T(8,128)(2,1)}, bf16[1152,256]{1,0:T(8,128)(2,1)S(1)}, u32[]{:S(2)}) copy-start(bf16[1152,256]{1,0:T(8,128)(2,1)S(1)} %reshape.298) | copy-start | bytes 1769476
  155.5 43.1 %copy-start.61 = (f32[128]{0:T(128)}, f32[128]{0:T(128)S(1)}, u32[]{:S(2)}) copy-start(f32[128]{0:T(128)S(1)} %multiply_power_fusion) | copy-start | bytes 1540
  156.2 42.4 %copy-start.47 = (f32[128]{0:T(128)}, f32[128]{0:T(128)S(1)}, u32[]{:S(2)}) copy-start(f32[128]{0:T(128)S(1)} %get-tuple-element.105) | copy-start | bytes 1540
  156.6 39.3 %copy-start.22 = (f32[128,256]{1,0:T(8,128)}, f32[128,256]{1,0:T(8,128)S(1)}, u32[]{:S(2)}) copy-start(f32[128,256]{1,0:T(8,128)S(1)} %get-tuple-element.115) | copy-start | bytes 393220
  158.2 46.1 %copy-start.26 = (f32[128,128]{1,0:T(8,128)}, f32[128,128]{1,0:T(8,128)S(1)}, u32[]{:S(2)}) copy-start(f32[128,128]{1,0:T(8,128)S(1)} %get-tuple-element.101) | copy-start | bytes 196612
  198.6 4.5 copy-start.1
  206.8 68.5 %copy-start.15 = (bf16[128,4,256]{0,2,1:T(8,128)(2,1)}, bf16[128,4,256]{0,2,1:T(8,128)(2,1)S(1)}, u32[]{:S(2)}) copy-start(bf16[128,4,256]{0,2,1:T(8,128)(2,1)S(1)} %fusion.23) | copy-start | bytes 786436
  206.8 4.1 copy-start.33
  210.9 64.5 %copy-start.57 = (f32[128]{0:T(128)}, f32[128]{0:T(128)S(1)}, u32[]{:S(2)}) copy-start(f32[128]{0:T(128)S(1)} %get-tuple-element.111) | copy-start | bytes 1540
  395.2 11.4 copy-start
  488.3 8.2 copy-start.12
  488.3 8.2 copy-start.41
  488.3 10.0 copy-start.4
  498.3 10.4 copy-start.24
  508.8 11.2 copy-start.9
  508.8 11.2 copy-start.34
  508.8 11.2 copy-start.58
  520.0 12.7 copy-start.7
  520.0 12.7 copy-start.54
  520.0 12.7 copy-start.67
  520.0 15.0 copy-start.66
  552.8 25.1 %copy-start.27 = (f32[128,128]{1,0:T(8,128)S(1)}, f32[128,128]{1,0:T(8,128)}, u32[]{:S(2)}) copy-start(f32[128,128]{1,0:T(8,128)} %copy-done.26) | copy-start | bytes 196612
  552.9 25.2 %copy-start.31 = (bf16[1024,256]{1,0:T(8,128)(2,1)S(1)}, bf16[1024,256]{1,0:T(8,128)(2,1)}, u32[]{:S(2)}) copy-start(bf16[1024,256]{1,0:T(8,128)(2,1)} %fusion.21) | copy-start | bytes 1572868
  552.9 25.2 %copy-start.32 = (bf16[1024,256]{1,0:T(8,128)(2,1)S(1)}, bf16[1024,256]{1,0:T(8,128)(2,1)}, u32[]{:S(2)}) copy-start(bf16[1024,256]{1,0:T(8,128)(2,1)} %fusion.20) | copy-start | bytes 1572868
  579.1 1587.3 %all-reduce.19.cloned.1.call-start = ((), (), s32[]{:S(2)}) async-start(), calls=%async_computation.7 | async-start | bytes 214695936
  580.9 30.1 %copy-start.60 = (f32[128]{0:T(128)S(1)}, f32[128]{0:T(128)}, u32[]{:S(2)}) copy-start(f32[128]{0:T(128)} %copy-done.59) | copy-start | bytes 1540
  581.0 30.1 %copy-start.62 = (f32[128]{0:T(128)S(1)}, f32[128]{0:T(128)}, u32[]{:S(2)}) copy-start(f32[128]{0:T(128)} %copy-done.61) | copy-start | bytes 1540
  581.0 30.4 %copy-start.23 = (f32[128,256]{1,0:T(8,128)S(1)}, f32[128,256]{1,0:T(8,128)}, u32[]{:S(2)}) copy-start(f32[128,256]{1,0:T(8,128)} %copy-done.22) | copy-start | bytes 393220
  581.0 30.4 %copy-start.50 = (f32[256]{0:T(256)S(1)}, f32[256]{0:T(256)}, u32[]{:S(2)}) copy-start(f32[256]{0:T(256)} %copy-done.49) | copy-start | bytes 3076
  581.0 30.4 %copy-start.56 = (f32[128]{0:T(128)S(1)}, f32[128]{0:T(128)}, u32[]{:S(2)}) copy-start(f32[128]{0:T(128)} %copy-done.55) | copy-start | bytes 1540
  581.0 30.6 %copy-start.65 = (f32[128]{0:T(128)S(1)}, f32[128]{0:T(128)}, u32[]{:S(2)}) copy-start(f32[128]{0:T(128)} %get-tuple-element.106) | copy-start | bytes 1540
  581.0 31.6 %copy-start.48 = (f32[128]{0:T(128)S(1)}, f32[128]{0:T(128)}, u32[]{:S(2)}) copy-start(f32[128]{0:T(128)} %copy-done.47) | copy-start | bytes 1540
  665.5 4.0 copy-start.44
  665.5 47.8 %copy-start.68 = (f32[128]{0:T(128)S(1)}, f32[128]{0:T(128)}, u32[]{:S(2)}) copy-start(f32[128]{0:T(128)} %get-tuple-element.104) | copy-start | bytes 1540
  666.4 46.9 %copy-start.11 = (f32[128,1152]{1,0:T(8,128)S(1)}, f32[128,1152]{1,0:T(8,128)}, u32[]{:S(2)}) copy-start(f32[128,1152]{1,0:T(8,128)} %copy-done.10) | copy-start | bytes 1769476
  (30 other events, 64.7 us)
Sparse Core Ops, SparseCore 0:
  10.9 60.5 all-gather.15
  74.5 56.8 all-gather.11
  134.4 122.4 all-gather.17
  259.7 116.8 all-gather.19
  379.3 108.8 all-gather.13
  579.2 30.8 reduce-scatter.1
  664.0 1502.4 all-reduce.18
where the time goes:
time: 2190 us; the launch traced here: 2180 us
  waiting for transfers between devices  1680 us (77%)
  blocking collectives  214 us (10%)
  matrix products  111 us (5%)
  other arithmetic  88 us (4%)
  local copies, waits for them, and re-layouts  72.2 us (3%)
    unnamed x8, waiting for transfers between devices  1460 us
    all_gather x1, waiting for transfers between devices, per_device(): lax.all_gather(up_weight, ('seq', 'ctx'), axis=0, tiled=True)  101 us
    unnamed x2, blocking collectives  82.6 us
    all_gather x1, waiting for transfers between devices, per_device(): lax.all_gather(down_weight, ('seq', 'ctx'), axis=0, tiled=True)  77 us
    unnamed x171, local copies, waits for them, and re-layouts  57.9 us
    concatenate x1, other arithmetic, per_device(): jnp.concatenate([transposed_times(normed, attention_backs), transposed_ti...  47.3 us
    all_gather x1, waiting for transfers between devices, per_device(): lax.all_gather(gate_weight, ('seq', 'ctx'), axis=0, tiled=True)  45.9 us
  transfers between devices with their start and end apart: 7, of which 5 were waited for; matrix products, arithmetic and copies ran while one was open for 5% of the time, Pallas kernels for 0%

commit v1 on v0

v1 whole, which is shorter than its diff:
```python
import math

import jax
import jax.numpy as jnp
from jax import lax
from jax.sharding import PartitionSpec as P

D = 1152
H = 4
DH = 256
FF = 6912


EPSILON = 1e-06
THETA = 1000000.0
GELU_COEF = math.sqrt(2.0 / math.pi)


def rms_factor(values):
    return lax.rsqrt(jnp.mean(values * values, axis=-1, keepdims=True) + EPSILON)


def norm_back(values, factor, gain_vector, upstream):
    scaled = gain_vector * upstream
    cubed = factor * factor * factor
    return factor * scaled - values * cubed * jnp.mean(scaled * values, axis=-1, keepdims=True)


def rotary(places):
    half_width = DH // 2
    exponent = jnp.arange(half_width, dtype=jnp.float32) * (-2.0 / DH)
    frequency = jnp.power(jnp.float32(THETA), exponent)
    angles = places.astype(jnp.float32)[:, None] * frequency[None, :]
    return (jnp.cos(angles), jnp.sin(angles))


def rotate(values, cosine, sinus):
    half_width = values.shape[-1] // 2
    first = values[..., :half_width]
    second = values[..., half_width:]
    return jnp.concatenate(
        [first * cosine - second * sinus, second * cosine + first * sinus], axis=-1
    )


def rotate_back(upstream, cosine, sinus):
    half_width = upstream.shape[-1] // 2
    first = upstream[..., :half_width]
    second = upstream[..., half_width:]
    return jnp.concatenate(
        [first * cosine + second * sinus, second * cosine - first * sinus], axis=-1
    )


def gelu_tanh(values):
    inner = GELU_COEF * (values + 0.044715 * values * values * values)
    return 0.5 * values * (1.0 + jnp.tanh(inner))


def gelu_slope(values):
    inner = GELU_COEF * (values + 0.044715 * values * values * values)
    tangent = jnp.tanh(inner)
    return 0.5 * (1.0 + tangent) + 0.5 * values * (1.0 - tangent * tangent) * GELU_COEF * (
        1.0 + 3.0 * 0.044715 * values * values
    )


def times_right(left_side, right_side):
    return jnp.dot(left_side, right_side, preferred_element_type=jnp.float32)


def times_transposed(left_side, right_side):
    return lax.dot_general(
        left_side, right_side, (((1,), (1,)), ((), ())), preferred_element_type=jnp.float32
    )


def transposed_times(left_side, right_side):
    return lax.dot_general(
        left_side, right_side, (((0,), (0,)), ((), ())), preferred_element_type=jnp.float32
    )


BOTH = ("seq", "ctx")


def to_heads(rows):
    return jnp.concatenate([rows[:, h * DH : (h + 1) * DH] for h in range(H)], axis=0)


def from_heads(stacked):
    count = stacked.shape[0] // H
    return jnp.concatenate([stacked[h * count : (h + 1) * count] for h in range(H)], axis=1)


def sum_to_owner(term):
    columns = term.shape[1]
    first = lax.psum_scatter(
        term.astype(jnp.bfloat16), "seq", scatter_dimension=0, tiled=True
    )
    ctx_total = lax.axis_size("ctx")
    own = first.shape[0] // ctx_total
    padded = -(-own // 16) * 16
    if padded != own:
        first = first.reshape(ctx_total, own, columns)
        first = jnp.pad(first, ((0, 0), (0, padded - own), (0, 0)))
        first = first.reshape(ctx_total * padded, columns)
    second = lax.psum_scatter(first, "ctx", scatter_dimension=0, tiled=True)
    return second[:own].astype(jnp.float32)


def per_device(
    inputs,
    positions,
    attention_gain,
    query_weight,
    key_weight,
    value_weight,
    query_gain,
    key_gain,
    output_weight,
    attention_post,
    feedfwd_gain,
    gate_weight,
    up_weight,
    down_weight,
    feedfwd_post,
    cotangent,
):
    seq_total = lax.axis_size("seq")
    ctx_total = lax.axis_size("ctx")
    device_total = seq_total * ctx_total
    token_count = inputs.shape[0]
    width_rows = query_weight.shape[0]
    head_rows = query_gain.shape[0]
    unit_rows = down_weight.shape[0]
    scaling = 1.0 / math.sqrt(DH)

    block_number = (positions[:1] // token_count).astype(jnp.bfloat16)
    small = jnp.concatenate(
        [attention_gain, attention_post, feedfwd_gain, feedfwd_post, query_gain, key_gain]
        + [block_number]
    )
    small_row = jnp.pad(small, (0, (H + 2) * DH - small.shape[0]))[None]
    packet = jnp.concatenate(
        [jnp.concatenate([query_weight, key_weight, value_weight], axis=1), small_row], axis=0
    )
    packets = lax.all_gather(packet, BOTH, axis=0, tiled=False)
    joint_weight = packets[:, :width_rows].reshape(D, (H + 2) * DH)
    smalls = packets[:, width_rows]

    def gain_of(start, size):
        return smalls[:, start : start + size].reshape(-1).astype(jnp.float32)

    gain_attention = gain_of(0, width_rows)
    gain_post = gain_of(width_rows, width_rows)
    gain_feed = gain_of(2 * width_rows, width_rows)
    gain_final = gain_of(3 * width_rows, width_rows)
    gain_query = gain_of(4 * width_rows, head_rows)
    gain_key = gain_of(4 * width_rows + head_rows, head_rows)
    numbers = smalls[:, 4 * width_rows + 2 * head_rows].astype(jnp.int32)
    own_numbers = lax.dynamic_slice(numbers, (lax.axis_index("seq") * ctx_total,), (ctx_total,))
    place_all = (
        own_numbers[:, None] * token_count + jnp.arange(token_count, dtype=jnp.int32)[None, :]
    ).reshape(-1)

    pair = jnp.stack([gate_weight, up_weight]).reshape(
        2, width_rows, seq_total, ctx_total, unit_rows
    )
    pair = jnp.transpose(pair, (3, 0, 1, 2, 4)).reshape(
        ctx_total, 2, width_rows, seq_total * unit_rows
    )
    pair = lax.all_to_all(pair, "ctx", 0, 0, tiled=False)
    unit_count = seq_total * unit_rows
    pair = jnp.transpose(pair, (1, 0, 2, 3)).reshape(2 * ctx_total * width_rows, unit_count)

    input_wide = inputs.astype(jnp.float32)
    input_factor = rms_factor(input_wide)
    normed = (input_wide * input_factor * gain_attention).astype(jnp.bfloat16)
    joint = times_right(normed, joint_weight)
    queries = to_heads(joint[:, : H * DH])
    key_rows = joint[:, H * DH : (H + 1) * DH]
    value_rows = joint[:, (H + 1) * DH :].astype(jnp.bfloat16)
    cosine, sinus = rotary(positions)
    cosine_heads = jnp.concatenate([cosine] * H, axis=0)
    sinus_heads = jnp.concatenate([sinus] * H, axis=0)
    query_factor = rms_factor(queries)
    query_rot = rotate(queries * query_factor * gain_query, cosine_heads, sinus_heads).astype(
        jnp.bfloat16
    )
    key_factor = rms_factor(key_rows)
    key_rot = rotate(key_rows * key_factor * gain_key, cosine, sinus).astype(jnp.bfloat16)
    both_rows = lax.all_gather(
        jnp.concatenate([key_rot, value_rows], axis=1), "ctx", axis=0, tiled=True
    )
    output_all = lax.all_gather(output_weight, BOTH, axis=0, tiled=True)
    both_rows, pair, down_own = lax.optimization_barrier((both_rows, pair, down_weight))
    pair_all = lax.all_gather(pair, "seq", axis=0, tiled=True).reshape(
        seq_total, 2, ctx_total * width_rows, unit_count
    )
    gate_all = pair_all[:, 0].reshape(D, unit_count)
    up_all = pair_all[:, 1].reshape(D, unit_count)
    down_all = lax.all_gather(down_own, "seq", axis=0, tiled=True)

    key_all = both_rows[:, :DH]
    value_all = both_rows[:, DH:]
    place_heads = jnp.concatenate([positions] * H, axis=0)
    allowed = place_all[None, :] <= place_heads[:, None]
    scores = times_transposed(query_rot, key_all) * scaling
    expscore = jnp.where(allowed, jnp.exp(scores), 0.0)
    weight_sum = jnp.sum(expscore, axis=-1, keepdims=True)
    summed = times_right(expscore.astype(jnp.bfloat16), value_all)
    attended_heads = (summed / weight_sum).astype(jnp.bfloat16)
    logsum = jnp.log(weight_sum)
    attended = from_heads(attended_heads)
    mixed_values = times_right(attended, output_all)
    mixed_factor = rms_factor(mixed_values)
    residual = input_wide + mixed_values * mixed_factor * gain_post
    residual_factor = rms_factor(residual)
    fed_own = (residual * residual_factor * gain_feed).astype(jnp.bfloat16)

    fed_rows = lax.all_gather(fed_own, "ctx", axis=0, tiled=True)
    gate_values = times_right(fed_rows, gate_all)
    up_values = times_right(fed_rows, up_all)
    hidden = (gelu_tanh(gate_values) * up_values).astype(jnp.bfloat16)
    down_values = lax.psum_scatter(
        times_right(hidden, down_all).astype(jnp.bfloat16), "ctx", scatter_dimension=0, tiled=True
    ).astype(jnp.float32)
    down_factor = rms_factor(down_values)
    block_out = (residual + down_values * down_factor * gain_final).astype(jnp.bfloat16)
    cot_wide = cotangent.astype(jnp.float32)
    grad_final = jnp.sum(cot_wide * down_values * down_factor, axis=0)
    down_back_own = norm_back(down_values, down_factor, gain_final, cot_wide).astype(jnp.bfloat16)
    down_back = lax.all_gather(down_back_own, "ctx", axis=0, tiled=True)
    hidden_back = times_transposed(down_back, down_all)
    gate_back = (hidden_back * up_values * gelu_slope(gate_values)).astype(jnp.bfloat16)
    up_back = (hidden_back * gelu_tanh(gate_values)).astype(jnp.bfloat16)
    fed_back = lax.psum_scatter(
        (times_transposed(gate_back, gate_all) + times_transposed(up_back, up_all)).astype(
            jnp.bfloat16
        ),
        "ctx",
        scatter_dimension=0,
        tiled=True,
    ).astype(jnp.float32)
    fed_back, late_hidden, late_down, late_fed, late_gate, late_up = lax.optimization_barrier(
        (fed_back, hidden, down_back, fed_rows, gate_back, up_back)
    )
    grad_down = lax.psum_scatter(
        transposed_times(late_hidden, late_down).astype(jnp.bfloat16),
        "seq",
        scatter_dimension=0,
        tiled=True,
    ).astype(jnp.float32)
    seq_rows = ctx_total * width_rows
    pair_term = jnp.stack(
        [
            transposed_times(late_fed, late_gate).astype(jnp.bfloat16).reshape(
                seq_total, seq_rows, unit_count
            ),
            transposed_times(late_fed, late_up).astype(jnp.bfloat16).reshape(
                seq_total, seq_rows, unit_count
            ),
        ],
        axis=1,
    ).reshape(seq_total * 2 * seq_rows, unit_count)
    pair_sum = lax.psum_scatter(pair_term, "seq", scatter_dimension=0, tiled=True)

    grad_feed = jnp.sum(fed_back * residual * residual_factor, axis=0)
    residual_back = cot_wide + norm_back(residual, residual_factor, gain_feed, fed_back)
    grad_post = jnp.sum(residual_back * mixed_values * mixed_factor, axis=0)
    mixed_back = norm_back(mixed_values, mixed_factor, gain_post, residual_back).astype(
        jnp.bfloat16
    )
    attended_back = to_heads(times_transposed(mixed_back, output_all))
    upper_round = attended_back.astype(jnp.bfloat16)
    row_delta = jnp.sum(attended_back * attended_heads.astype(jnp.float32), axis=-1, keepdims=True)
    probability = jnp.where(allowed, jnp.exp(scores - logsum), 0.0)
    value_terms = transposed_times(probability.astype(jnp.bfloat16), upper_round)
    prob_back = times_transposed(upper_round, value_all)
    score_back = (probability * (prob_back - row_delta) * scaling).astype(jnp.bfloat16)
    query_rot_back = times_right(score_back, key_all)
    key_terms = transposed_times(score_back, query_rot)
    own_rows = lax.psum_scatter(
        jnp.concatenate([key_terms, value_terms], axis=1).astype(jnp.bfloat16),
        "ctx",
        scatter_dimension=0,
        tiled=True,
    ).astype(jnp.float32)
    grad_output = sum_to_owner(transposed_times(attended, mixed_back))
    key_rot_back = own_rows[:, :DH]
    value_back = own_rows[:, DH:].astype(jnp.bfloat16)
    query_up = rotate_back(query_rot_back, cosine_heads, sinus_heads)
    grad_qgain = jnp.sum(query_up * queries * query_factor, axis=0)
    query_back = from_heads(
        norm_back(queries, query_factor, gain_query, query_up).astype(jnp.bfloat16)
    )
    key_up = rotate_back(key_rot_back, cosine, sinus)
    grad_kgain = jnp.sum(key_up * key_rows * key_factor, axis=0)
    key_back = norm_back(key_rows, key_factor, gain_key, key_up).astype(jnp.bfloat16)
    joint_back = jnp.concatenate([query_back, key_back, value_back], axis=1)
    normed_back = times_transposed(joint_back, joint_weight)
    grad_attention = jnp.sum(normed_back * input_wide * input_factor, axis=0)
    input_grad = residual_back + norm_back(input_wide, input_factor, gain_attention, normed_back)
    grad_joint = sum_to_owner(transposed_times(normed, joint_back))
    grad_query = grad_joint[:, : H * DH]
    grad_key = grad_joint[:, H * DH : (H + 1) * DH]
    grad_value = grad_joint[:, (H + 1) * DH :]
    pair_back = jnp.transpose(
        pair_sum.reshape(2, ctx_total, width_rows, unit_count), (1, 0, 2, 3)
    )
    pair_back = lax.all_to_all(pair_back, "ctx", 0, 0, tiled=False)
    pair_back = jnp.transpose(
        pair_back.reshape(ctx_total, 2, width_rows, seq_total, unit_rows), (1, 2, 3, 0, 4)
    ).reshape(2, width_rows, FF)
    grad_gate = pair_back[0].astype(jnp.float32)
    grad_up = pair_back[1].astype(jnp.float32)
    gains_summed = tuple(
        lax.psum_scatter(term, BOTH, scatter_dimension=0, tiled=True)
        for term in (grad_attention, grad_qgain, grad_kgain, grad_post, grad_feed, grad_final)
    )
    return (
        block_out,
        input_grad,
        gains_summed[0],
        grad_query,
        grad_key,
        grad_value,
        gains_summed[1],
        gains_summed[2],
        grad_output,
        gains_summed[3],
        gains_summed[4],
        grad_gate,
        grad_up,
        grad_down,
        gains_summed[5],
    )


def solution(mesh):
    return jax.shard_map(
        per_device,
        mesh=mesh,
        in_specs=(
            P(("seq", "ctx"), None),
            P(("seq", "ctx")),
            P(("seq", "ctx")),
            P(("seq", "ctx"), None),
            P(("seq", "ctx"), None),
            P(("seq", "ctx"), None),
            P(("seq", "ctx")),
            P(("seq", "ctx")),
            P(("seq", "ctx"), None),
            P(("seq", "ctx")),
            P(("seq", "ctx")),
            P(("seq", "ctx"), None),
            P(("seq", "ctx"), None),
            P(("seq", "ctx"), None),
            P(("seq", "ctx")),
            P(("seq", "ctx"), None),
        ),
        out_specs=(
            P(("seq", "ctx"), None),
            P(("seq", "ctx"), None),
            P(("seq", "ctx")),
            P(("seq", "ctx"), None),
            P(("seq", "ctx"), None),
            P(("seq", "ctx"), None),
            P(("seq", "ctx")),
            P(("seq", "ctx")),
            P(("seq", "ctx"), None),
            P(("seq", "ctx")),
            P(("seq", "ctx")),
            P(("seq", "ctx"), None),
            P(("seq", "ctx"), None),
            P(("seq", "ctx"), None),
            P(("seq", "ctx")),
        ),
        check_vma=False,
    )
```

time: 2190 us -> 744 us (0.34)
  waiting for transfers between devices: 1680 us -> 423 us
  blocking collectives: 214 us -> 73 us
  matrix products: 111 us -> 72.9 us
  other arithmetic: 88 us -> 52 us
    unnamed x8 -> x17, waiting for transfers between devices: 1460 us -> 1.93 us
    reduce_scatter x0 -> x7, waiting for transfers between devices: none -> 197 us  [the longest x1 50.6 us: per_device(): lax.psum_scatter(pair_term, 'seq', scatter_dimension=0, tiled=True)]
    all_gather x5 -> x0, blocking collectives: 131 us -> none  [the longest x1 43.6 us: per_device(): lax.all_gather(key_weight, ('seq', 'ctx'), axis=0, tiled=True)]
    concatenate x3 -> x2, other arithmetic: 72.2 us -> 2.09 us  [the longest x1 1.51 us: per_device(): jnp.concatenate([key_rot, value_rows], axis=1)]
    unnamed x171 -> x131, local copies, waits for them, and re-layouts: 57.9 us -> 12.5 us
    unnamed x2 -> x1, blocking collectives: 82.6 us -> 41.9 us
    all_to_all x0 -> x1, blocking collectives: none -> 31 us  [per_device(): pair = lax.all_to_all(pair, 'ctx', 0, 0, tiled=False)]
    all_gather x5 -> x7, waiting for transfers between devices: 224 us -> 202 us  [the longest x1 60.4 us: per_device(): packets = lax.all_gather(packet, BOTH, axis=0, tiled=False)]
  transfers between devices with their start and end apart: 7 -> 17, of which waited for: 5 -> 13; matrix products, arithmetic and copies ran while one was open for 5% -> 20% of each run, Pallas kernels for 0% -> 0%
where the time goes in v1:
time: 744 us; the launch traced here: 734 us
  waiting for transfers between devices  423 us (57%)
  local copies, waits for them, and re-layouts  88 us (12%)
  blocking collectives  73 us (10%)
  matrix products  72.9 us (10%)
  other arithmetic  52 us (7%)
  between operations  17.7 us (2%)
    all_gather x1, waiting for transfers between devices, per_device(): packets = lax.all_gather(packet, BOTH, axis=0, tiled=False)  60.4 us
    reduce_scatter x1, waiting for transfers between devices, per_device(): lax.psum_scatter(pair_term, 'seq', scatter_dimension=0, tiled=True)  50.6 us
    all_gather x1, waiting for transfers between devices, per_device(): lax.all_gather(pair, 'seq', axis=0, tiled=True)  46.7 us
    reduce_scatter x2, waiting for transfers between devices, sum_to_owner(): lax.psum_scatter(term.astype(jnp.bfloat16), 'seq', scatter_dimension=0, t...  45.8 us
    unnamed x1, blocking collectives  41.9 us
    reduce_scatter x1, waiting for transfers between devices, per_device(): lax.psum_scatter(times_right(hidden, down_all).astype(jnp.bfloat16), 'ctx...  35.7 us
    reduce_scatter x1, waiting for transfers between devices, per_device(): lax.psum_scatter((times_transposed(gate_back, gate_all) + times_transpose...  35 us
    all_to_all x1, blocking collectives, per_device(): pair = lax.all_to_all(pair, 'ctx', 0, 0, tiled=False)  31 us
  transfers between devices with their start and end apart: 17, of which 13 were waited for; matrix products, arithmetic and copies ran while one was open for 20% of the time, Pallas kernels for 0%

profile of v1, /device:TPU:0, one launch (start us, length us, event | category | flops | bytes accessed | tf_op | source)
XLA Modules:
  0.0 733.5 jit_solution(17822556028523004603)
XLA Ops:
  9.8 4.1 concatenate.52
  19.0 60.4 %all-gather.22.cloned.1.call-done = bf16[32,37,1536]{2,1,0:T(8,128)(2,1)} async-done(((bf16[1,37,1536]{2,1,0:T(8,128)(2,1)}), bf16[32,37,1536]{2,1,0:T(8,128)(2,1)}) %all-gather.22.cloned.1.call-update) | async-done | bytes 3637264 | tf_op jit(solution)/shard_map/all_gather | solution.py:148
  82.3 3.9 reshape.264
  96.7 3.7 stack.12
  100.4 2.2 copy.113
  102.5 3.7 stack.13
  107.6 3.0 maximum_bitcast_fusion
  110.6 3.3 reshape.265
  115.9 31.0 %all_to_all.10 = bf16[8,2,36,864]{3,1,2,0:T(2,128)(2,1)S(1)} all-to-all(bf16[8,2,36,864]{3,1,2,0:T(2,128)(2,1)S(1)} %copy.115), channel_id=1, replica_groups=mesh['seq'=4,'ctx'=8] {'ctx'}, dimensions={0} | all-to-all | bytes 1990656 | tf_op jit(solution)/shard_map/all_to_all | solution.py:173
  148.1 2.3 reshape.266
  164.8 13.1 %all-gather.12.cloned.1.call-done = bf16[1024,1152]{1,0:T(8,128)(2,1)} async-done(((bf16[32,1152]{1,0:T(8,128)(2,1)}), bf16[1024,1152]{1,0:T(8,128)(2,1)}) %all-gather.12.cloned.1.call-update) | async-done | bytes 2359312 | tf_op jit(solution)/shard_map/all_gather | solution.py:196
  178.0 2.5 multiply_reduce_fusion.5
  184.4 46.7 %all-gather.16.cloned.1.call-done = bf16[2304,864]{1,0:T(8,128)(2,1)} async-done(((bf16[576,864]{1,0:T(8,128)(2,1)}), bf16[2304,864]{1,0:T(8,128)(2,1)}) %all-gather.16.cloned.1.call-update) | async-done | bytes 3981328 | tf_op jit(solution)/shard_map/all_gather | solution.py:198
  231.1 4.5 fusion.78
  235.6 29.1 %all-gather.14.cloned.1.call-done = bf16[1024,1152]{1,0:T(8,128)(2,1)} async-done(((bf16[128,1152]{1,0:T(8,128)(2,1)}), bf16[1024,1152]{1,0:T(8,128)(2,1)}) %all-gather.14.cloned.1.call-update) | async-done | bytes 2359312 | tf_op jit(solution)/shard_map/all_gather | solution.py:222
  264.6 5.0 fusion.83
  271.4 5.7 multiply_convert_fusion.1
  277.1 22.8 %all-gather.18.cloned.1.call-done = bf16[864,1152]{1,0:T(8,128)(2,1)} async-done(((bf16[216,1152]{1,0:T(8,128)(2,1)}), bf16[864,1152]{1,0:T(8,128)(2,1)}) %all-gather.18.cloned.1.call-update) | async-done | bytes 1990672 | tf_op jit(solution)/shard_map/all_gather | solution.py:203
  299.9 6.4 convolution_convert_fusion.2
  307.8 35.7 %reduce-scatter.12.cloned.1.call-done = bf16[128,1152]{1,0:T(8,128)(2,1)} async-done(((bf16[1024,1152]{1,0:T(8,128)(2,1)}), bf16[128,1152]{1,0:T(8,128)(2,1)}) %reduce-scatter.12.cloned.1.call-update) | async-done | bytes 294928 | tf_op jit(solution)/shard_map/reduce_scatter | solution.py:226
  349.1 29.9 %all-gather.20.cloned.1.call-done = bf16[1024,1152]{1,0:T(8,128)(2,1)} async-done(((bf16[128,1152]{1,0:T(8,128)(2,1)}), bf16[1024,1152]{1,0:T(8,128)(2,1)}) %all-gather.20.cloned.1.call-update) | async-done | bytes 2359312 | tf_op jit(solution)/shard_map/all_gather | solution.py:234
  379.0 8.9 %multiply_convert_fusion = (bf16[1024,864]{0,1:T(8,128)(2,1)S(1)}, bf16[1024,864]{0,1:T(8,128)(2,1)S(1)}) fusion(f32[1024,864]{0,1:T(8,128)} %copy-done.57, f32[1024,864]{0,1:T(8,128)} %get-tuple-element.107, bf16[1024,1152]{1,0:T(8,128)(2,1)} %all-gather.20.cloned.1.call-done, bf16[864,1152]{1,0:T(8,128)(2,1)} %all-gather.18.cloned.1.call-done), kind=kOutput, calls=%fused_computation.14 | convolution fusion | flops 2058780672 | bytes 14966784 | tf_op jit(solution)/shard_map/dot_general | solution.py:73
  388.0 2.9 fusion.84
  391.0 4.3 add_convert_fusion
  396.8 35.0 %reduce-scatter.14.cloned.1.call-done = bf16[128,1152]{1,0:T(8,128)(2,1)} async-done(((bf16[1024,1152]{1,0:T(8,128)(2,1)}), bf16[128,1152]{1,0:T(8,128)(2,1)}) %reduce-scatter.14.cloned.1.call-update) | async-done | bytes 294928 | tf_op jit(solution)/shard_map/reduce_scatter | solution.py:238
  434.9 2.7 multiply_reduce_fusion.1
  444.0 3.3 convolution_convert_fusion.1
  453.1 22.4 %reduce-scatter.16.cloned.1.call-done = bf16[128,512]{1,0:T(8,128)(2,1)} async-done(((bf16[1024,512]{1,0:T(8,128)(2,1)}), bf16[128,512]{1,0:T(8,128)(2,1)}) %reduce-scatter.16.cloned.1.call-update) | async-done | bytes 131088 | tf_op jit(solution)/shard_map/reduce_scatter | solution.py:284
  482.2 4.1 convolution_convert_fusion
  486.6 6.0 convolution_convert_fusion.4
  492.5 4.1 copy.125
  496.7 6.0 convolution_convert_fusion.3
  502.6 4.1 copy.126
  506.8 2.7 pad_maximum_fusion
  509.5 2.3 copy.127
  511.9 6.0 convolution_convert_fusion.5
  518.6 45.8 %reduce-scatter.18.cloned.1.call-done = bf16[288,1536]{1,0:T(8,128)(2,1)} async-done(((bf16[1152,1536]{1,0:T(8,128)(2,1)}), bf16[288,1536]{1,0:T(8,128)(2,1)}) %reduce-scatter.18.cloned.1.call-update) | async-done | bytes 884752 | tf_op jit(solution)/shard_map/reduce_scatter | solution.py:98
  566.5 2.4 pad.9
  568.9 50.6 %reduce-scatter.26.cloned.1.call-done = bf16[576,864]{1,0:T(8,128)(2,1)} async-done(((bf16[2304,864]{1,0:T(8,128)(2,1)}), bf16[576,864]{1,0:T(8,128)(2,1)}) %reduce-scatter.26.cloned.1.call-update) | async-done | bytes 995344 | tf_op jit(solution)/shard_map/reduce_scatter | solution.py:267
  619.6 2.2 reshape.271
  621.7 3.3 copy.128
  625.0 4.6 all-to-all-start.1
  629.6 3.7 fusion.41
  633.4 41.9 %all-reduce.9 = (f32[1152]{0:T(1024)S(1)}, f32[256]{0:T(256)S(1)}, f32[256]{0:T(256)S(1)}, f32[1152]{0:T(1024)S(1)}, f32[1152]{0:T(1024)S(1)}, /*index=5*/f32[1152]{0:T(1024)S(1)}) all-reduce(f32[1152]{0:T(1024)} %get-tuple-element.41, f32[256]{0:T(256)} %get-tuple-element.37, ...), channel_id=6, replica_groups=mesh['seq'=4,'ctx'=8] {'seq','ctx'}, use_global_device_ids=true, to_apply=%region_18.19.clone | all-reduce | flops 5120 | bytes 40960
  679.4 2.4 fusion.38
  683.9 7.3 reduce-scatter.24.cloned.1.call-done
  692.8 3.9 reshape.285
  701.9 22.6 %reduce-scatter.20.cloned.1.call-done = bf16[48,1536]{1,0:T(8,128)(2,1)} async-done(((bf16[384,1536]{1,0:T(8,128)(2,1)}), bf16[48,1536]{1,0:T(8,128)(2,1)}) %reduce-scatter.20.cloned.1.call-update) | async-done | bytes 147472 | tf_op jit(solution)/shard_map/reduce_scatter | solution.py:108
  (250 shorter events, 91.2 us)
Async XLA Ops:
  7.2 72.2 %all-gather.22.cloned.1.call-start = ((), (), s32[]{:S(2)}) async-start(), calls=%async_computation.25 | async-start | bytes 4055040 | tf_op jit(solution)/shard_map/all_gather | solution.py:148
  15.6 134.8 %all-gather.10.cloned.1.call-start = ((), (), s32[]{:S(2)}) async-start(), calls=%async_computation.11 | async-start | bytes 1179648 | tf_op jit(solution)/shard_map/all_gather | solution.py:193
  19.0 67.2 %copy-start.37 = (f32[128]{0:T(128)}, f32[128]{0:T(128)S(1)}, u32[]{:S(2)}) copy-start(f32[128]{0:T(128)S(1)} %get-tuple-element.93) | copy-start | bytes 1540
  90.0 12.6 %copy-start.38 = (f32[128]{0:T(128)}, f32[128]{0:T(128)S(1)}, u32[]{:S(2)}) copy-start(f32[128]{0:T(128)S(1)} %get-tuple-element.95) | copy-start | bytes 1540
  90.8 11.8 %copy-start.33 = (f32[256]{0:T(256)}, f32[256]{0:T(256)S(1)}, u32[]{:S(2)}) copy-start(f32[256]{0:T(256)S(1)} %reshape.275) | copy-start | bytes 3076
  95.9 82.1 %all-gather.12.cloned.1.call-start = ((), (), s32[]{:S(2)}) async-start(), calls=%async_computation.12 | async-start | bytes 2433024 | tf_op jit(solution)/shard_map/all_gather | solution.py:196
  96.6 134.5 %all-gather.16.cloned.1.call-start = ((), (), s32[]{:S(2)}) async-start(), calls=%async_computation.14 | async-start | bytes 5160960 | tf_op jit(solution)/shard_map/all_gather | solution.py:198
  148.1 2.4 copy-start.49
  150.4 114.2 %all-gather.14.cloned.1.call-start = ((), (), s32[]{:S(2)}) async-start(), calls=%async_computation.13 | async-start | bytes 2654208 | tf_op jit(solution)/shard_map/all_gather | solution.py:222
  156.0 5.2 copy-start.18
  156.0 5.2 copy-start.20
  156.0 5.3 copy-start.45
  156.1 5.3 copy-start.52
  158.3 3.9 copy-start.43
  178.0 3.1 copy-start
  178.0 4.7 copy-start.25
  183.5 116.4 %all-gather.18.cloned.1.call-start = ((), (), s32[]{:S(2)}) async-start(), calls=%async_computation.15 | async-start | bytes 2488320 | tf_op jit(solution)/shard_map/all_gather | solution.py:203
  184.1 159.4 %reduce-scatter.12.cloned.1.call-start = ((), (), s32[]{:S(2)}) async-start(), calls=%async_computation.16 | async-start | bytes 2654208 | tf_op jit(solution)/shard_map/reduce_scatter | solution.py:226
  264.6 6.7 copy-start.15
  264.6 6.7 copy-start.51
  306.3 72.7 %all-gather.20.cloned.1.call-start = ((), (), s32[]{:S(2)}) async-start(), calls=%async_computation.17 | async-start | bytes 2654208 | tf_op jit(solution)/shard_map/all_gather | solution.py:234
  348.6 83.2 %reduce-scatter.14.cloned.1.call-start = ((), (), s32[]{:S(2)}) async-start(), calls=%async_computation.18 | async-start | bytes 2654208 | tf_op jit(solution)/shard_map/reduce_scatter | solution.py:238
  379.0 9.0 %copy-start.17 = (bf16[4,1,288,864]{3,2,1,0:T(8,128)(2,1)S(1)}, bf16[4,1,288,864]{3,2,1,0:T(8,128)(2,1)}, u32[]{:S(2)}) copy-start(bf16[4,1,288,864]{3,2,1,0:T(8,128)(2,1)} %get-tuple-element.56) | copy-start | bytes 5971972
  388.0 3.0 copy-start.58
  388.0 3.0 copy-start.59
  388.0 3.0 copy-start.16
  395.3 80.2 %reduce-scatter.16.cloned.1.call-start = ((), (), s32[]{:S(2)}) async-start(), calls=%async_computation.19 | async-start | bytes 1179648 | tf_op jit(solution)/shard_map/reduce_scatter | solution.py:284
  431.8 3.0 copy-start.3
  431.8 3.0 copy-start.5
  431.8 3.0 copy-start.7
  431.8 3.0 copy-start.14
  432.9 4.7 copy-start.40
  432.9 4.6 copy-start.50
  434.8 2.9 copy-start.1
  443.9 74.1 %reduce-scatter.22.cloned.1.call-start = ((), (), s32[]{:S(2)}) async-start(), calls=%async_computation.22 | async-start | bytes 2949120 | tf_op jit(solution)/shard_map/reduce_scatter | solution.py:98
  447.3 2.2 copy-start.31
  447.3 117.1 %reduce-scatter.18.cloned.1.call-start = ((), (), s32[]{:S(2)}) async-start(), calls=%async_computation.20 | async-start | bytes 4423680 | tf_op jit(solution)/shard_map/reduce_scatter | solution.py:98
  447.3 2.1 copy-start.9
  447.3 2.1 copy-start.10
  447.4 2.1 copy-start.11
  447.4 2.9 copy-start.36
  449.4 28.1 %copy-start.34 = (f32[256]{0:T(256)S(1)}, f32[256]{0:T(256)}, u32[]{:S(2)}) copy-start(f32[256]{0:T(256)} %copy-done.33) | copy-start | bytes 3076
  486.3 133.2 %reduce-scatter.26.cloned.1.call-start = ((), (), s32[]{:S(2)}) async-start(), calls=%async_computation.24 | async-start | bytes 5160960 | tf_op jit(solution)/shard_map/reduce_scatter | solution.py:267
  511.8 170.1 %reduce-scatter.28.cloned.1.call-start = ((), (), s32[]{:S(2)}) async-start(), calls=%async_computation.26 | async-start | bytes 2488320
  517.9 173.3 %reduce-scatter.24.cloned.1.call-start = ((), (), s32[]{:S(2)}) async-start(), calls=%async_computation.23 | async-start | bytes 663552 | tf_op jit(solution)/shard_map/reduce_scatter | solution.py:108
  518.5 206.0 %reduce-scatter.20.cloned.1.call-start = ((), (), s32[]{:S(2)}) async-start(), calls=%async_computation.21 | async-start | bytes 1327104 | tf_op jit(solution)/shard_map/reduce_scatter | solution.py:108
  625.0 67.8 %all-to-all-start.1 = ((bf16[8,2,36,864]{3,1,2,0:T(2,128)(2,1)}), bf16[8,2,36,864]{3,1,2,0:T(2,128)(2,1)}, u32[]{:S(2)}, u32[]{:S(2)}) async-start(bf16[8,2,36,864]{3,1,2,0:T(2,128)(2,1)} %copy.128), calls=%async_computation.9 | async-start | bytes 2064384 | tf_op jit(solution)/shard_map/all_to_all | solution.py:312
  629.6 3.7 copy-start.32
  (29 other events, 35.0 us)
Sparse Core Ops, SparseCore 0:
  15.7 63.6 all-gather.21
  96.0 21.0 all-gather.9
  120.2 57.7 all-gather.11
  180.2 50.8 all-gather.15
  233.2 31.4 all-gather.13
  266.3 33.5 all-gather.17
  306.5 37.0 reduce-scatter.11
  348.7 30.3 all-gather.19
  395.4 36.3 reduce-scatter.13
  444.1 31.4 reduce-scatter.15
  478.6 35.5 reduce-scatter.21
  517.1 47.1 reduce-scatter.17
  567.5 52.0 reduce-scatter.25
  622.4 35.0 reduce-scatter.27
  659.6 31.5 reduce-scatter.23
  693.4 31.0 reduce-scatter.19
